TPU v7x, 32 devices: a whole 2x2x4 slice. The times are simulated.
32 devices in a mesh: rep: 8 (over z, core), rows: 4 (over y, x).
Axes of the slice: x: 2, y: 2, z: 4, core: 2. Of those that a mesh axis runs over, the one named last changes fastest.
Arguments:
- weights: bfloat16 [7168, 2048], P('rows'), may hold values from -6 to 6
- momentum: float32 [8, 7168, 2048], P('rep', 'rows'), may hold values from -8 to 8
- gradient: bfloat16 [8, 7168, 2048], P('rep', 'rows'), may hold values from -8 to 8
- right_factor: float32 [2048, 512], P('rows'), may hold values from -6 to 6
Outputs:
- new_weights: bfloat16 [7168, 2048], P('rows')
- new_momentum: float32 [8, 7168, 2048], P('rep', 'rows')
- new_right: float32 [2048, 512], P('rows')
All inputs are finite; a program needn't handle non-finite values.
Results may differ from a plain program's by a relative error of at most 0.019.
Values may be sent and summed in bfloat16 or wider, within the bound.
A program may use at most 128 MiB of HBM per device.

v0:
```python
import jax
import jax.numpy as jnp
from jax import lax
from jax.sharding import PartitionSpec as P

M = 7168
N = 2048
momentum_keep = 0.05
learn_rate = 0.5
tiny = 1e-06


def per_device(weights, momentum, gradient, right_factor):
    groups = lax.axis_size("rep")
    shards = lax.axis_size("rows")
    combined = momentum[0] + gradient[0].astype(jnp.float32)
    combined_half = combined.astype(jnp.bfloat16)
    columns = combined.shape[1]
    share = columns // shards
    left_local = jnp.dot(
        combined_half,
        lax.all_gather(right_factor.astype(jnp.bfloat16), "rows", axis=0, tiled=True),
        preferred_element_type=jnp.float32,
    )
    left_local = lax.optimization_barrier(left_local.astype(jnp.bfloat16)).astype(jnp.float32)
    left_mean = lax.psum(left_local.astype(jnp.bfloat16), "rep").astype(jnp.float32) / groups
    gram = lax.psum(jnp.dot(left_mean.T, left_mean, precision=lax.Precision.HIGHEST), "rows")
    chol = jnp.linalg.cholesky(gram)
    left_orth = jax.scipy.linalg.solve_triangular(chol, left_mean.T, lower=True).T
    left_half = left_orth.astype(jnp.bfloat16)
    partial_right = jnp.einsum(
        "ij,ik->jk", combined_half, left_half, preferred_element_type=jnp.float32
    )
    right_mean = lax.psum(partial_right, ("rep", "rows")) / groups
    normed = right_mean / jnp.sqrt(jnp.mean(right_mean * right_mean, axis=0) + tiny)
    feedback = jnp.dot(
        left_half, right_mean.astype(jnp.bfloat16).T, preferred_element_type=jnp.float32
    )
    update = jnp.dot(left_half, normed.astype(jnp.bfloat16).T, preferred_element_type=jnp.float32)
    new_right = lax.dynamic_slice_in_dim(normed, lax.axis_index("rows") * share, share, 0)
    new_momentum = combined - momentum_keep * feedback
    new_weights = (weights.astype(jnp.float32) - learn_rate * jnp.sqrt(M / N) * update).astype(
        jnp.bfloat16
    )
    return (new_weights, new_momentum[None], new_right)


def solution(mesh):
    in_specs = (P("rows", None), P("rep", "rows", None), P("rep", "rows", None), P("rows", None))
    out_specs = (P("rows", None), P("rep", "rows", None), P("rows", None))
    return jax.shard_map(
        per_device, mesh=mesh, in_specs=in_specs, out_specs=out_specs, check_vma=False
    )
```

profile of v0, /device:TPU:0, one launch (start us, length us, event | category | flops | bytes accessed | tf_op | source)
XLA Modules:
  0.0 525.9 jit_solution(10342217912073874617)
XLA Ops:
  7.2 2.1 convert_element_type.35
  9.4 39.0 %all-gather.2.cloned.1.call-done = bf16[2048,512]{1,0:T(8,128)(2,1)} async-done(((bf16[512,512]{1,0:T(8,128)(2,1)}), bf16[2048,512]{1,0:T(8,128)(2,1)}) %all-gather.2.cloned.1.call-update) | async-done | bytes 2097168 | tf_op jit(solution)/shard_map/all_gather | solution.py:22
  48.3 13.1 %convolution_convert_fusion = bf16[1792,512]{1,0:T(8,128)(2,1)} fusion(bf16[2048,512]{1,0:T(8,128)(2,1)} %all-gather.2.cloned.1.call-done, f32[1,1792,2048]{2,1,0:T(8,128)} %param.5, bf16[1,1792,2048]{2,1,0:T(8,128)(2,1)} %param.6), kind=kOutput, calls=%fused_computation.13 | convolution fusion | flops 3770023936 | bytes 25952256 | tf_op jit(solution)/shard_map/dot_general | solution.py:20
  61.5 63.3 %all-reduce.5.cloned.1.call-done = bf16[1792,512]{1,0:T(8,128)(2,1)} async-done(((bf16[1792,512]{1,0:T(8,128)(2,1)}), bf16[1792,512]{1,0:T(8,128)(2,1)}) %all-reduce.5.cloned.1.call-update) | async-done | bytes 1835024 | tf_op jit(solution)/shard_map/psum | solution.py:26
  124.7 9.4 %fusion.2 = f32[512,512]{0,1:T(8,128)} fusion(bf16[1792,512]{1,0:T(8,128)(2,1)} %all-reduce.5.cloned.1.call-done), kind=kOutput, calls=%fused_computation.12 | convolution fusion | flops 5638979584 | bytes 2883584 | tf_op jit(solution)/shard_map/dot_general | solution.py:27
  134.4 2.4 fusion.1
  136.8 50.0 %all-reduce.7.cloned.1.call-done = f32[512,512]{0,1:T(8,128)} async-done(((f32[512,512]{0,1:T(8,128)}), f32[512,512]{0,1:T(8,128)}) %all-reduce.7.cloned.1.call-update) | async-done | bytes 1048592 | tf_op jit(solution)/shard_map/psum | solution.py:27
  186.8 1.6 copy.8
  188.3 1.4 fusion.18
  189.8 11.7 %cholesky.104 = f32[128,128]{1,0:T(8,128)S(1)} custom-call(f32[128,128]{1,0:T(8,128)S(1)} %cholesky.266), custom_call_target="Cholesky" | custom-call | tf_op jit(solution)/shard_map/jit(cholesky)/cholesky | solution.py:28
  201.5 9.8 %custom-call.31 = f32[1,128,128]{1,2,0:T(8,128)S(1)} custom-call(f32[1,128,128]{2,1,0:T(8,128)S(1)} %get-tuple-element.30), custom_call_target="InvertDiagBlocksLowerTriangular" | custom-call | tf_op jit(solution)/shard_map/jit(cholesky)/cholesky | solution.py:28
  212.2 11.7 %cholesky.217 = f32[128,128]{1,0:T(8,128)S(1)} custom-call(f32[128,128]{1,0:T(8,128)S(1)} %cholesky.270), custom_call_target="Cholesky" | custom-call | tf_op jit(solution)/shard_map/jit(cholesky)/cholesky | solution.py:28
  223.9 10.2 %custom-call.32 = f32[1,128,128]{1,2,0:T(8,128)S(1)} custom-call(f32[1,128,128]{2,1,0:T(8,128)S(1)} %get-tuple-element.27), custom_call_target="InvertDiagBlocksLowerTriangular" | custom-call | tf_op jit(solution)/shard_map/jit(cholesky)/cholesky | solution.py:28
  234.8 11.7 %cholesky.238 = f32[128,128]{1,0:T(8,128)S(1)} custom-call(f32[128,128]{1,0:T(8,128)S(1)} %cholesky.275), custom_call_target="Cholesky" | custom-call | tf_op jit(solution)/shard_map/jit(cholesky)/cholesky | solution.py:28
  247.3 9.8 %custom-call.33 = f32[1,128,128]{1,2,0:T(8,128)S(1)} custom-call(f32[1,128,128]{2,1,0:T(8,128)S(1)} %get-tuple-element.24), custom_call_target="InvertDiagBlocksLowerTriangular" | custom-call | tf_op jit(solution)/shard_map/jit(cholesky)/cholesky | solution.py:28
  257.7 11.9 %cholesky.255 = f32[128,128]{1,0:T(8,128)S(1)} custom-call(f32[128,128]{1,0:T(8,128)S(1)} %convolution_subtract_fusion.4), custom_call_target="Cholesky" | custom-call | tf_op jit(solution)/shard_map/jit(cholesky)/cholesky | solution.py:28
  273.6 8.5 %while.1 = (s32[]{:T(128)}, f32[512,512]{1,0:T(8,128)S(1)}, s32[4,2]{0,1:T(2,128)S(1)}, f32[4,128,128]{2,1,0:T(8,128)S(1)}, s32[]{:T(128)}) while((s32[]{:T(128)}, f32[512,512]{1,0:T(8,128)S(1)}, s32[4,2]{0,1:T(2,128)S(1)}, f32[4,128,128]{2,1,0:T(8,128)S(1)}, s32[]{:T(128)}) %tuple.34), condition=%wide.while_cond, body=%wide.while_body.sunk | while | flops 2 | bytes 131181 | solution.py:29
  274.3 1.4 bitcast_dynamic-update-slice_fusion.2
  276.4 1.4 bitcast_dynamic-update-slice_fusion.2
  278.5 1.4 bitcast_dynamic-update-slice_fusion.2
  280.6 1.4 bitcast_dynamic-update-slice_fusion.2
  282.1 39.3 %custom-call.34 = f32[4,128,128]{1,2,0:T(8,128)S(1)} custom-call(f32[4,128,128]{2,1,0:T(8,128)S(1)} %get-tuple-element.10), custom_call_target="InvertDiagBlocksLowerTriangular" | custom-call | tf_op jit(solution)/shard_map/jit(_solve_triangular)/triangular_solve | solution.py:29
  321.4 2.3 fusion.45
  323.7 2.8 convolution_subtract_fusion.1
  327.5 3.2 convolution_subtract_fusion
  331.7 4.7 fusion.9
  336.3 1.2 convolution_convert_fusion.1
  338.3 11.3 %fusion.41 = f32[2048,512]{1,0:T(8,128)} fusion(f32[1,1792,2048]{2,1,0:T(8,128)} %param.5, bf16[1,1792,2048]{2,1,0:T(8,128)(2,1)S(1)} %bitcast.67, bf16[128,1792]{1,0:T(8,128)(2,1)S(1)} %convolution_convert_fusion.1, bf16[128,1792]{1,0:T(8,128)(2,1)S(1)} %get-tuple-element.33, bf16[128,1792]{1,0:T(8,128)(2,1)S(1)} %get-tuple-element.35, ...), kind=kOutput, calls=%fused_computation.86 | convolution fusion | flops 3776446464 | bytes 28049408 | tf_op jit(solution)/shard_map/ij,ik->jk/dot_general | solution.py:31
  349.6 142.5 %all-reduce.9.cloned.1.call-done = f32[2048,512]{1,0:T(8,128)} async-done(((f32[2048,512]{1,0:T(8,128)}), f32[2048,512]{1,0:T(8,128)}) %all-reduce.9.cloned.1.call-update) | async-done | bytes 4194320 | tf_op jit(solution)/shard_map/psum | solution.py:34
  492.1 2.9 multiply_reduce_fusion
  496.7 8.2 %subtract_convert_fusion = bf16[1792,2048]{1,0:T(8,128)(2,1)} fusion(bf16[1792,2048]{1,0:T(8,128)(2,1)} %param.4, f32[2048,512]{1,0:T(8,128)S(1)} %multiply_divide_fusion, bf16[128,1792]{1,0:T(8,128)(2,1)S(1)} %copy-done.6, bf16[128,1792]{1,0:T(8,128)(2,1)S(1)} %copy-done.4, bf16[128,1792]{1,0:T(8,128)(2,1)S(1)} %get-tuple-element.35, ...), kind=kOutput, calls=%fused_computation.5 | convolution fusion | flops 3781165056 | bytes 20709376 | tf_op jit(solution)/shard_map/dot_general | solution.py:39
  506.0 13.0 %fusion = f32[1,1792,2048]{2,1,0:T(8,128)} fusion(f32[1,1792,2048]{2,1,0:T(8,128)} %param.5, bf16[1,1792,2048]{2,1,0:T(8,128)(2,1)} %param.6, f32[2048,512]{1,0:T(8,128)S(1)} %copy-done, bf16[128,1792]{1,0:T(8,128)(2,1)} %copy-done.5, bf16[128,1792]{1,0:T(8,128)(2,1)} %copy-done.3, bf16[128,1792]{1,0:T(8,128)(2,1)S(1)} %get-tuple-element.35, ...), kind=kOutput, calls=%fused_computation.4 | convolution fusion | flops 3782213632 | bytes 42729472 | tf_op jit(solution)/shard_map/dot_general | solution.py:36
  (61 shorter events, 12.9 us)
Async XLA Ops:
  7.2 41.2 %all-gather.2.cloned.1.call-start = ((), (), s32[]{:S(2)}) async-start(), calls=%async_computation | async-start | bytes 2621440 | tf_op jit(solution)/shard_map/all_gather | solution.py:22
  9.3 115.4 %all-reduce.5.cloned.1.call-start = ((), (), s32[]{:S(2)}) async-start(), calls=%async_computation.1 | async-start | bytes 3670016 | tf_op jit(solution)/shard_map/psum | solution.py:26
  61.4 125.4 %all-reduce.7.cloned.1.call-start = ((), (), s32[]{:S(2)}) async-start(), calls=%async_computation.2 | async-start | bytes 2097152 | tf_op jit(solution)/shard_map/psum | solution.py:27
  124.7 9.7 %copy-start.2 = (bf16[1792,512]{1,0:T(8,128)(2,1)S(1)}, bf16[1792,512]{1,0:T(8,128)(2,1)}, u32[]{:S(2)}) copy-start(bf16[1792,512]{1,0:T(8,128)(2,1)} %all-reduce.5.cloned.1.call-done) | copy-start | bytes 5505028
  134.1 358.0 %all-reduce.9.cloned.1.call-start = ((), (), s32[]{:S(2)}) async-start(), calls=%async_computation.3 | async-start | bytes 8388608 | tf_op jit(solution)/shard_map/psum | solution.py:34
  321.4 6.1 %copy-start.1 = (f32[512,1792]{0,1:T(8,128)S(1)}, f32[512,1792]{0,1:T(8,128)}, u32[]{:S(2)}) copy-start(f32[512,1792]{0,1:T(8,128)} %fusion.1) | copy-start | bytes 11010052
  326.5 11.8 %slice-start = ((s8[7340032]{0:T(1024)(128)(4,1)}), s8[4194304]{0:T(1024)(128)(4,1)S(1)}, s32[]{:S(2)}) async-start(s8[7340032]{0:T(1024)(128)(4,1)} %bitcast.66), calls=%async_computation.4 | async-start | bytes 8388608
  330.7 7.6 %slice-start.1 = ((s8[7340032]{0:T(1024)(128)(4,1)}), s8[3145728]{0:T(1024)(128)(4,1)S(1)}, s32[]{:S(2)}) async-start(s8[7340032]{0:T(1024)(128)(4,1)} %bitcast.66), calls=%async_computation.5 | async-start | bytes 6291456
  331.7 17.9 %copy-start.3 = (bf16[128,1792]{1,0:T(8,128)(2,1)}, bf16[128,1792]{1,0:T(8,128)(2,1)S(1)}, u32[]{:S(2)}) copy-start(bf16[128,1792]{1,0:T(8,128)(2,1)S(1)} %get-tuple-element.33) | copy-start | bytes 1376260
  337.5 0.8 copy-start.5
  492.1 3.4 copy-start
  495.6 1.0 copy-start.4
  495.6 1.2 copy-start.6
Sparse Core Ops, SparseCore 0:
  10.4 37.8 all-gather.1
  61.5 63.1 all-reduce.4
  134.3 52.4 all-reduce.6
  349.7 142.3 all-reduce.8
where the time goes:
time: 534 us; the launch traced here: 526 us
  waiting for transfers between devices  295 us (55%)
  other arithmetic  128 us (24%)
  matrix products  72.8 us (14%)
  between operations  17 us (3%)
  local copies, waits for them, and re-layouts  13.1 us (2%)
    psum x1, waiting for transfers between devices, per_device(): right_mean = lax.psum(partial_right, ('rep', 'rows')) / groups  143 us
    another operation x14, other arithmetic, per_device(): chol = jnp.linalg.cholesky(gram)  79 us
    psum x1, waiting for transfers between devices, per_device(): lax.psum(left_local.astype(jnp.bfloat16), 'rep').astype(jnp.float32)  63.3 us
    psum x1, waiting for transfers between devices, per_device(): lax.psum(jnp.dot(left_mean.T, left_mean, precision=lax.Precision.HIGHEST)...  50 us
    another operation x3, other arithmetic, per_device(): jax.scipy.linalg.solve_triangular(chol, left_mean.T, lower=True)  39.4 us
    all_gather x1, waiting for transfers between devices, per_device(): lax.all_gather(right_factor.astype(jnp.bfloat16), 'rows', axis=0, tiled=T...  39 us
    another operation x7, matrix products, per_device(): jax.scipy.linalg.solve_triangular(chol, left_mean.T, lower=True)  16 us
    dot_general x1, matrix products, per_device(): jnp.dot(combined_half, lax.all_gather(right_factor.astype(jnp.bfloat16),...  13.1 us
  transfers between devices with their start and end apart: 4, of which 4 were waited for; matrix products, arithmetic and copies ran while one was open for 0% of the time, Pallas kernels for 0%

commit v1 on v0

--- a/solution.py
+++ b/solution.py
@@ -31,7 +31,7 @@
     partial_right = jnp.einsum(
         "ij,ik->jk", combined_half, left_half, preferred_element_type=jnp.float32
     )
-    right_mean = lax.psum(partial_right, ("rep", "rows")) / groups
+    right_mean = lax.psum(lax.psum(partial_right, "rows"), "rep") / groups
     normed = right_mean / jnp.sqrt(jnp.mean(right_mean * right_mean, axis=0) + tiny)
     feedback = jnp.dot(
         left_half, right_mean.astype(jnp.bfloat16).T, preferred_element_type=jnp.float32

time: 534 us -> 594 us (1.11)
  waiting for transfers between devices: 295 us -> 355 us
    psum x1 -> x2, waiting for transfers between devices: 143 us -> 202 us  [per_device(): right_mean = lax.psum(lax.psum(partial_right, 'rows'), 'rep') / groups]
  transfers between devices with their start and end apart: 4 -> 5, of which waited for: 4 -> 5; matrix products, arithmetic and copies ran while one was open for 0% -> 0% of each run, Pallas kernels for 0% -> 0%
where the time goes in v1:
time: 594 us; the launch traced here: 586 us
  waiting for transfers between devices  355 us (60%)
  other arithmetic  128 us (22%)
  matrix products  72.8 us (12%)
  between operations  17 us (3%)
  local copies, waits for them, and re-layouts  13.2 us (2%)
    psum x2, waiting for transfers between devices, per_device(): right_mean = lax.psum(lax.psum(partial_right, 'rows'), 'rep') / groups  202 us
    another operation x14, other arithmetic, per_device(): chol = jnp.linalg.cholesky(gram)  79 us
    psum x1, waiting for transfers between devices, per_device(): lax.psum(left_local.astype(jnp.bfloat16), 'rep').astype(jnp.float32)  63.3 us
    psum x1, waiting for transfers between devices, per_device(): lax.psum(jnp.dot(left_mean.T, left_mean, precision=lax.Precision.HIGHEST)...  50 us
    another operation x3, other arithmetic, per_device(): jax.scipy.linalg.solve_triangular(chol, left_mean.T, lower=True)  39.4 us
    all_gather x1, waiting for transfers between devices, per_device(): lax.all_gather(right_factor.astype(jnp.bfloat16), 'rows', axis=0, tiled=T...  39 us
    another operation x7, matrix products, per_device(): jax.scipy.linalg.solve_triangular(chol, left_mean.T, lower=True)  16 us
    dot_general x1, matrix products, per_device(): jnp.dot(combined_half, lax.all_gather(right_factor.astype(jnp.bfloat16),...  13.1 us
  transfers between devices with their start and end apart: 5, of which 5 were waited for; matrix products, arithmetic and copies ran while one was open for 0% of the time, Pallas kernels for 0%

profile of v1, /device:TPU:0, one launch (start us, length us, event | category | flops | bytes accessed | tf_op | source)
XLA Modules:
  0.0 585.9 jit_solution(6376913870071803371)
XLA Ops:
  7.2 2.1 convert_element_type.35
  9.4 39.0 %all-gather.2.cloned.1.call-done = bf16[2048,512]{1,0:T(8,128)(2,1)} async-done(((bf16[512,512]{1,0:T(8,128)(2,1)}), bf16[2048,512]{1,0:T(8,128)(2,1)}) %all-gather.2.cloned.1.call-update) | async-done | bytes 2097168 | tf_op jit(solution)/shard_map/all_gather | solution.py:22
  48.3 13.1 %convolution_convert_fusion = bf16[1792,512]{1,0:T(8,128)(2,1)} fusion(bf16[2048,512]{1,0:T(8,128)(2,1)} %all-gather.2.cloned.1.call-done, f32[1,1792,2048]{2,1,0:T(8,128)} %param.5, bf16[1,1792,2048]{2,1,0:T(8,128)(2,1)} %param.6), kind=kOutput, calls=%fused_computation.13 | convolution fusion | flops 3770023936 | bytes 25952256 | tf_op jit(solution)/shard_map/dot_general | solution.py:20
  61.5 63.3 %all-reduce.6.cloned.1.call-done = bf16[1792,512]{1,0:T(8,128)(2,1)} async-done(((bf16[1792,512]{1,0:T(8,128)(2,1)}), bf16[1792,512]{1,0:T(8,128)(2,1)}) %all-reduce.6.cloned.1.call-update) | async-done | bytes 1835024 | tf_op jit(solution)/shard_map/psum | solution.py:26
  124.7 9.4 %fusion.2 = f32[512,512]{0,1:T(8,128)} fusion(bf16[1792,512]{1,0:T(8,128)(2,1)} %all-reduce.6.cloned.1.call-done), kind=kOutput, calls=%fused_computation.12 | convolution fusion | flops 5638979584 | bytes 2883584 | tf_op jit(solution)/shard_map/dot_general | solution.py:27
  134.4 2.4 fusion.1
  136.8 50.0 %all-reduce.8.cloned.1.call-done = f32[512,512]{0,1:T(8,128)} async-done(((f32[512,512]{0,1:T(8,128)}), f32[512,512]{0,1:T(8,128)}) %all-reduce.8.cloned.1.call-update) | async-done | bytes 1048592 | tf_op jit(solution)/shard_map/psum | solution.py:27
  186.8 1.6 copy.8
  188.3 1.4 fusion.18
  189.8 11.7 %cholesky.104 = f32[128,128]{1,0:T(8,128)S(1)} custom-call(f32[128,128]{1,0:T(8,128)S(1)} %cholesky.266), custom_call_target="Cholesky" | custom-call | tf_op jit(solution)/shard_map/jit(cholesky)/cholesky | solution.py:28
  201.5 9.8 %custom-call.31 = f32[1,128,128]{1,2,0:T(8,128)S(1)} custom-call(f32[1,128,128]{2,1,0:T(8,128)S(1)} %get-tuple-element.30), custom_call_target="InvertDiagBlocksLowerTriangular" | custom-call | tf_op jit(solution)/shard_map/jit(cholesky)/cholesky | solution.py:28
  212.2 11.7 %cholesky.217 = f32[128,128]{1,0:T(8,128)S(1)} custom-call(f32[128,128]{1,0:T(8,128)S(1)} %cholesky.270), custom_call_target="Cholesky" | custom-call | tf_op jit(solution)/shard_map/jit(cholesky)/cholesky | solution.py:28
  223.9 10.2 %custom-call.32 = f32[1,128,128]{1,2,0:T(8,128)S(1)} custom-call(f32[1,128,128]{2,1,0:T(8,128)S(1)} %get-tuple-element.27), custom_call_target="InvertDiagBlocksLowerTriangular" | custom-call | tf_op jit(solution)/shard_map/jit(cholesky)/cholesky | solution.py:28
  234.8 11.7 %cholesky.238 = f32[128,128]{1,0:T(8,128)S(1)} custom-call(f32[128,128]{1,0:T(8,128)S(1)} %cholesky.275), custom_call_target="Cholesky" | custom-call | tf_op jit(solution)/shard_map/jit(cholesky)/cholesky | solution.py:28
  247.3 9.8 %custom-call.33 = f32[1,128,128]{1,2,0:T(8,128)S(1)} custom-call(f32[1,128,128]{2,1,0:T(8,128)S(1)} %get-tuple-element.24), custom_call_target="InvertDiagBlocksLowerTriangular" | custom-call | tf_op jit(solution)/shard_map/jit(cholesky)/cholesky | solution.py:28
  257.7 11.9 %cholesky.255 = f32[128,128]{1,0:T(8,128)S(1)} custom-call(f32[128,128]{1,0:T(8,128)S(1)} %convolution_subtract_fusion.4), custom_call_target="Cholesky" | custom-call | tf_op jit(solution)/shard_map/jit(cholesky)/cholesky | solution.py:28
  273.6 8.5 %while.1 = (s32[]{:T(128)}, f32[512,512]{1,0:T(8,128)S(1)}, s32[4,2]{0,1:T(2,128)S(1)}, f32[4,128,128]{2,1,0:T(8,128)S(1)}, s32[]{:T(128)}) while((s32[]{:T(128)}, f32[512,512]{1,0:T(8,128)S(1)}, s32[4,2]{0,1:T(2,128)S(1)}, f32[4,128,128]{2,1,0:T(8,128)S(1)}, s32[]{:T(128)}) %tuple.34), condition=%wide.while_cond, body=%wide.while_body.sunk | while | flops 2 | bytes 131181 | solution.py:29
  274.3 1.4 bitcast_dynamic-update-slice_fusion.2
  276.4 1.4 bitcast_dynamic-update-slice_fusion.2
  278.5 1.4 bitcast_dynamic-update-slice_fusion.2
  280.6 1.4 bitcast_dynamic-update-slice_fusion.2
  282.1 39.3 %custom-call.34 = f32[4,128,128]{1,2,0:T(8,128)S(1)} custom-call(f32[4,128,128]{2,1,0:T(8,128)S(1)} %get-tuple-element.10), custom_call_target="InvertDiagBlocksLowerTriangular" | custom-call | tf_op jit(solution)/shard_map/jit(_solve_triangular)/triangular_solve | solution.py:29
  321.4 2.3 fusion.45
  323.7 2.8 convolution_subtract_fusion.1
  327.5 3.2 convolution_subtract_fusion
  331.7 4.7 fusion.9
  338.4 11.3 %fusion.41 = f32[2048,512]{1,0:T(8,128)} fusion(f32[1,1792,2048]{2,1,0:T(8,128)} %param.5, bf16[1,1792,2048]{2,1,0:T(8,128)(2,1)S(1)} %bitcast.67, bf16[128,1792]{1,0:T(8,128)(2,1)S(1)} %convolution_convert_fusion.1, bf16[128,1792]{1,0:T(8,128)(2,1)S(1)} %get-tuple-element.33, bf16[128,1792]{1,0:T(8,128)(2,1)S(1)} %get-tuple-element.35, ...), kind=kOutput, calls=%fused_computation.86 | convolution fusion | flops 3776446464 | bytes 28049408 | tf_op jit(solution)/shard_map/ij,ik->jk/dot_general | solution.py:31
  349.7 103.7 %all-reduce.10.cloned.1.call-done = f32[2048,512]{1,0:T(8,128)} async-done(((f32[2048,512]{1,0:T(8,128)}), f32[2048,512]{1,0:T(8,128)}) %all-reduce.10.cloned.1.call-update) | async-done | bytes 4194320 | tf_op jit(solution)/shard_map/psum | solution.py:34
  453.5 98.7 %all-reduce.12.cloned.1.call-done = f32[2048,512]{1,0:T(8,128)} async-done(((f32[2048,512]{1,0:T(8,128)}), f32[2048,512]{1,0:T(8,128)}) %all-reduce.12.cloned.1.call-update) | async-done | bytes 4194320 | tf_op jit(solution)/shard_map/psum | solution.py:34
  552.2 2.9 multiply_reduce_fusion
  556.8 8.2 %subtract_convert_fusion = bf16[1792,2048]{1,0:T(8,128)(2,1)} fusion(bf16[1792,2048]{1,0:T(8,128)(2,1)} %param.4, f32[2048,512]{1,0:T(8,128)S(1)} %multiply_divide_fusion, bf16[128,1792]{1,0:T(8,128)(2,1)S(1)} %copy-done.6, bf16[128,1792]{1,0:T(8,128)(2,1)S(1)} %copy-done.4, bf16[128,1792]{1,0:T(8,128)(2,1)S(1)} %get-tuple-element.35, ...), kind=kOutput, calls=%fused_computation.5 | convolution fusion | flops 3781165056 | bytes 20709376 | tf_op jit(solution)/shard_map/dot_general | solution.py:39
  566.0 13.0 %fusion = f32[1,1792,2048]{2,1,0:T(8,128)} fusion(f32[1,1792,2048]{2,1,0:T(8,128)} %param.5, bf16[1,1792,2048]{2,1,0:T(8,128)(2,1)} %param.6, f32[2048,512]{1,0:T(8,128)S(1)} %copy-done, bf16[128,1792]{1,0:T(8,128)(2,1)} %copy-done.5, bf16[128,1792]{1,0:T(8,128)(2,1)} %copy-done.3, bf16[128,1792]{1,0:T(8,128)(2,1)S(1)} %get-tuple-element.35, ...), kind=kOutput, calls=%fused_computation.4 | convolution fusion | flops 3782213632 | bytes 42729472 | tf_op jit(solution)/shard_map/dot_general | solution.py:36
  (64 shorter events, 14.2 us)
Async XLA Ops:
  7.2 41.2 %all-gather.2.cloned.1.call-start = ((), (), s32[]{:S(2)}) async-start(), calls=%async_computation | async-start | bytes 2621440 | tf_op jit(solution)/shard_map/all_gather | solution.py:22
  9.3 115.4 %all-reduce.6.cloned.1.call-start = ((), (), s32[]{:S(2)}) async-start(), calls=%async_computation.1 | async-start | bytes 3670016 | tf_op jit(solution)/shard_map/psum | solution.py:26
  61.4 125.4 %all-reduce.8.cloned.1.call-start = ((), (), s32[]{:S(2)}) async-start(), calls=%async_computation.2 | async-start | bytes 2097152 | tf_op jit(solution)/shard_map/psum | solution.py:27
  124.7 9.7 %copy-start.2 = (bf16[1792,512]{1,0:T(8,128)(2,1)S(1)}, bf16[1792,512]{1,0:T(8,128)(2,1)}, u32[]{:S(2)}) copy-start(bf16[1792,512]{1,0:T(8,128)(2,1)} %all-reduce.6.cloned.1.call-done) | copy-start | bytes 5505028
  134.1 319.3 %all-reduce.10.cloned.1.call-start = ((), (), s32[]{:S(2)}) async-start(), calls=%async_computation.3 | async-start | bytes 8388608 | tf_op jit(solution)/shard_map/psum | solution.py:34
  321.4 6.1 %copy-start.1 = (f32[512,1792]{0,1:T(8,128)S(1)}, f32[512,1792]{0,1:T(8,128)}, u32[]{:S(2)}) copy-start(f32[512,1792]{0,1:T(8,128)} %fusion.1) | copy-start | bytes 11010052
  326.5 11.8 %slice-start = ((s8[7340032]{0:T(1024)(128)(4,1)}), s8[4194304]{0:T(1024)(128)(4,1)S(1)}, s32[]{:S(2)}) async-start(s8[7340032]{0:T(1024)(128)(4,1)} %bitcast.66), calls=%async_computation.5 | async-start | bytes 8388608
  330.7 7.7 %slice-start.1 = ((s8[7340032]{0:T(1024)(128)(4,1)}), s8[3145728]{0:T(1024)(128)(4,1)S(1)}, s32[]{:S(2)}) async-start(s8[7340032]{0:T(1024)(128)(4,1)} %bitcast.66), calls=%async_computation.6 | async-start | bytes 6291456
  331.7 18.0 %copy-start.3 = (bf16[128,1792]{1,0:T(8,128)(2,1)}, bf16[128,1792]{1,0:T(8,128)(2,1)S(1)}, u32[]{:S(2)}) copy-start(bf16[128,1792]{1,0:T(8,128)(2,1)S(1)} %get-tuple-element.33) | copy-start | bytes 1376260
  337.5 0.8 copy-start.5
  349.7 202.5 %all-reduce.12.cloned.1.call-start = ((), (), s32[]{:S(2)}) async-start(), calls=%async_computation.4 | async-start | bytes 8388608 | tf_op jit(solution)/shard_map/psum | solution.py:34
  552.2 3.4 copy-start
  555.6 1.0 copy-start.4
  555.6 1.2 copy-start.6
Sparse Core Ops, SparseCore 0:
  10.4 37.8 all-gather.1
  61.5 63.1 all-reduce.5
  134.3 52.4 all-reduce.7
  349.8 103.6 all-reduce.9
  455.6 96.4 all-reduce.11
